TPU v7x, 256 devices: a whole 4x4x8 slice. The times are simulated.
256 devices in a mesh: grp: 8 (over y, z_lo), dev: 32 (over x, z_hi, core).
Axes of the slice: x: 4, y: 4, z: 8 (z_hi: 4, z_lo: 2; z = z_hi * 2 + z_lo), core: 2. Of those that a mesh axis runs over, the one named last changes fastest.
Arguments:
- resid: bfloat16 [32768, 1536], P(('grp', 'dev')), may hold values from -1.5 to 1.5
- queries: bfloat16 [32768, 1536], P(('grp', 'dev')), may hold values from -6 to 6
- suffix_kv: bfloat16 [32768, 2, 512], P(('grp', 'dev')), may hold values from -6 to 6
- prefix_kv: bfloat16 [8, 2048, 2, 512], P('grp', 'dev'), may hold values from -6 to 6
- segments: int32 [256, 128], P(('grp', 'dev')), may hold values from 0 to 3, never falling along the last dimension, each value on 1 to 64 neighbouring positions
- o_weight: bfloat16 [1536, 1536], P(('grp', 'dev')), may hold values from -0.15625 to 0.15625
- norm_gain: float32 [1536], replicated, may hold values from 0.25 to 1.75
- router: bfloat16 [1536, 32], replicated, may hold values from -0.15625 to 0.15625
- routes: int32 [32768, 8], P(('grp', 'dev')), may hold values from 0 to 31, all different within a row; in each aligned block of 128 rows (0 to 127, 128 to 255, ...) at most 48 rows name the same one
- w_gate_up: bfloat16 [32, 1536, 1024], P('dev', 'grp'), may hold values from -0.15625 to 0.15625
- w_down: bfloat16 [32, 512, 1536], P('dev', 'grp'), may hold values from -0.25 to 0.25
Outputs:
- layer_out: bfloat16 [32768, 1536], P(('grp', 'dev'))
Inputs may be any that keep to these rules, and one draw needn't show every extreme that they name: At most 48 of one device's routes name one expert.
All inputs are finite; a program needn't handle non-finite values.
Results may differ from a plain program's by a relative error of at most 0.012.
Values may be sent and summed in bfloat16 or wider, within the bound.
A program may use at most 128 MiB of HBM per device.

v0:
```python
import jax
import jax.numpy as jnp
from jax import lax
from jax.sharding import PartitionSpec as P

D = 1536
HEADS = 24
KVH = 8
HDIM = 64
FFE = 512
TOPK = 8
EXPERTS = 32
ATT = 1536
CAP = 48


def per_device(
    resid,
    queries,
    suffix_kv,
    prefix_kv,
    segments,
    o_weight,
    norm_gain,
    router,
    routes,
    w_gate_up,
    w_down,
):
    tok_rows = resid.shape[0]
    ratio = HEADS // KVH
    scale = 1.0 / HDIM**0.5
    query_heads = queries.reshape(tok_rows, KVH, ratio, HDIM)

    def update(carry, keys, values, mask):
        running, totals, accum = carry
        count = keys.shape[0]
        scores = (
            jnp.einsum(
                "tgrd,ngd->grtn",
                query_heads,
                keys.reshape(count, KVH, HDIM),
                preferred_element_type=jnp.float32,
            )
            * scale
        )
        if mask is not None:
            scores = jnp.where(mask[None, None], scores, jnp.float32(-1e30))
        newmax = jnp.maximum(running, jnp.max(scores, axis=-1))
        factor = jnp.exp(running - newmax)
        weights = jnp.exp(scores - newmax[..., None])
        totals = totals * factor + jnp.sum(weights, axis=-1)
        accum = accum * factor[..., None] + jnp.einsum(
            "grtn,ngd->grtd",
            weights.astype(jnp.bfloat16),
            values.reshape(count, KVH, HDIM),
            preferred_element_type=jnp.float32,
        )
        return (newmax, totals, accum)

    initial = (
        jnp.full((KVH, ratio, tok_rows), -1e30, jnp.float32),
        jnp.zeros((KVH, ratio, tok_rows), jnp.float32),
        jnp.zeros((KVH, ratio, tok_rows, HDIM), jnp.float32),
    )
    piece = lax.all_gather(prefix_kv[0], "dev", axis=0, tiled=True)
    carry = update(initial, piece[:, 0], piece[:, 1], None)
    seg_row = segments[0]
    positions = jnp.arange(tok_rows, dtype=jnp.int32)
    local_mask = (seg_row[:, None] == seg_row[None, :]) & (positions[None, :] <= positions[:, None])
    running, totals, accum = update(carry, suffix_kv[:, 0], suffix_kv[:, 1], local_mask)
    attended = (
        (accum / totals[..., None])
        .transpose(2, 0, 1, 3)
        .reshape(tok_rows, ATT)
        .astype(jnp.bfloat16)
    )
    projected = jnp.dot(
        attended,
        lax.all_gather(o_weight, ("grp", "dev"), axis=0, tiled=True),
        preferred_element_type=jnp.float32,
    )
    hidden = resid.astype(jnp.float32) + projected
    inverse = lax.rsqrt(jnp.mean(hidden * hidden, axis=-1, keepdims=True) + 1e-06)
    normed = (hidden * inverse * norm_gain).astype(jnp.bfloat16)
    logits = jnp.dot(normed, router, preferred_element_type=jnp.float32)
    expert_ids = jnp.arange(EXPERTS, dtype=jnp.int32)
    onehot = routes[:, :, None] == expert_ids[None, None, :]
    chosen = jnp.sum(jnp.where(onehot, logits[:, None, :], 0.0), axis=-1)
    sig = jax.nn.sigmoid(chosen)
    gates = (sig / jnp.sum(sig, axis=-1, keepdims=True)).astype(jnp.bfloat16)
    flat = onehot.reshape(tok_rows * TOPK, EXPERTS).astype(jnp.int32)
    before = jnp.cumsum(flat, axis=0) - flat
    slot = jnp.sum(before * flat, axis=-1).reshape(tok_rows, TOPK)
    place = routes * CAP + slot
    slot_ids = jnp.arange(EXPERTS * CAP, dtype=jnp.int32)
    hits = place[None, :, :] == slot_ids[:, None, None]
    table = jnp.sum(hits.astype(jnp.float32), axis=-1).astype(jnp.bfloat16)
    dispatch = jnp.dot(table, normed, preferred_element_type=jnp.float32).astype(jnp.bfloat16)
    dispatch = dispatch.reshape(EXPERTS, CAP, D)
    slot_count = dispatch.shape[1]
    received = lax.all_to_all(dispatch, "dev", split_axis=0, concat_axis=1, tiled=True)
    sliced = received
    gate_up = jnp.einsum(
        "erd,edf->erf",
        sliced,
        lax.all_gather(w_gate_up, "grp", axis=1, tiled=True),
        preferred_element_type=jnp.float32,
    )
    act = (jax.nn.silu(gate_up[..., :FFE]) * gate_up[..., FFE:]).astype(jnp.bfloat16)
    sliced = act
    expert_out = jnp.einsum(
        "erf,efd->erd",
        sliced,
        lax.all_gather(w_down, "grp", axis=1, tiled=True),
        preferred_element_type=jnp.float32,
    ).astype(jnp.bfloat16)
    returned = lax.all_to_all(expert_out, "dev", split_axis=1, concat_axis=0, tiled=True)
    returned = returned.reshape(EXPERTS * slot_count, D)
    back_hits = place[:, :, None] == slot_ids[None, None, :]
    ctable = jnp.sum(
        jnp.where(back_hits, gates[:, :, None].astype(jnp.float32), 0.0), axis=1
    ).astype(jnp.bfloat16)
    mixed = jnp.dot(ctable, returned, preferred_element_type=jnp.float32)
    return (hidden + mixed).astype(jnp.bfloat16)


def solution(mesh):
    return jax.shard_map(
        per_device,
        mesh=mesh,
        in_specs=(
            P(("grp", "dev"), None),
            P(("grp", "dev"), None),
            P(("grp", "dev"), None, None),
            P("grp", "dev", None, None),
            P(("grp", "dev"), None),
            P(("grp", "dev"), None),
            P(),
            P(),
            P(("grp", "dev"), None),
            P("dev", "grp", None),
            P("dev", "grp", None),
        ),
        out_specs=P(("grp", "dev"), None),
        check_vma=False,
    )
```

profile of v0, /device:TPU:1, one launch (start us, length us, event | category | flops | bytes accessed | tf_op | source)
XLA Modules:
  0.0 973.9 jit_solution(531432880128900151)
XLA Ops:
  7.4 0.7 all-gather.11.cloned.1.call-update
  8.1 0.7 all-gather.13.cloned.1.call-update
  8.8 0.8 copy.98
  9.6 0.1 eq.85
  9.7 0.1 eq.81
  9.8 1.2 copy.92
  11.0 1.5 fusion.54
  12.5 0.2 copy.95
  12.7 0.2 copy.96
  12.9 9.0 reduce-window.6
  21.9 0.1 slice.34
  22.0 0.1 copy.100
  22.3 0.1 broadcast_add_fusion
  22.6 0.7 multiply_add_fusion
  23.3 8.0 convert_reduce_fusion
  31.4 1.6 fusion.55
  33.0 42.5 %all-gather.11.cloned.1.call-done = bf16[1,2048,2,512]{3,2,0,1:T(2,128)(2,1)} async-done(((bf16[1,64,2,512]{3,2,0,1:T(2,128)(2,1)}), bf16[1,2048,2,512]{3,2,0,1:T(2,128)(2,1)}) %all-gather.11.cloned.1.call-update) | async-done | bytes 4194320 | tf_op jit(solution)/shard_map/all_gather | solution.py:66
  75.5 9.9 %fusion.53 = (bf16[2048,1,512]{2,1,0:T(2,128)(2,1)}, bf16[2048,1,512]{2,1,0:T(2,128)(2,1)}) fusion(bf16[2048,2,512]{2,1,0:T(2,128)(2,1)} %bitcast.137), kind=kLoop, calls=%fused_computation.72 | loop fusion | bytes 8388608 | tf_op jit(solution)/shard_map/slice | solution.py:67
  85.4 10.6 %copy.93 = bf16[2048,1,512]{0,2,1:T(8,128)(2,1)} copy(bf16[2048,1,512]{2,1,0:T(2,128)(2,1)} %get-tuple-element.8) | data formatting | bytes 4194304 | tf_op jit(solution)/shard_map/slice | solution.py:67
  96.0 9.0 copy.91
  105.0 10.1 %bitcast_reduce_fusion = (f32[8,3,128]{2,1,0:T(4,128)S(1)}, f32[8,2048,128,3]{2,1,3,0:T(8,128)}) fusion(bf16[2048,8,64,1]{0,2,3,1:T(8,128)(2,1)S(1)} %bitcast.138, bf16[128,8,3,64]{0,3,2,1:T(8,128)(2,1)S(1)} %bitcast.142), kind=kOutput, calls=%fused_computation.1 | convolution fusion | flops 817886208 | bytes 27668480 | tf_op jit(solution)/shard_map/tgrd,ngd->grtn/dot_general | solution.py:39
  115.1 0.3 fusion.20
  115.4 10.6 %fusion.1 = f32[8,3,128]{2,1,0:T(4,128)S(1)} fusion(f32[8,2048,128,3]{2,1,3,0:T(8,128)} %get-tuple-element.17, f32[8,3,128]{2,1,0:T(4,128)S(1)} %get-tuple-element.13), kind=kLoop, calls=%fused_computation.3 | loop fusion | flops 18871296 | bytes 25190400 | tf_op jit(solution)/shard_map/reduce_sum | solution.py:52
  126.1 10.5 %fusion.30 = f32[128,8,3,64]{0,3,2,1:T(8,128)S(1)} fusion(bf16[2048,8,64,1]{0,2,3,1:T(8,128)(2,1)S(1)} %bitcast.140, f32[8,2048,128,3]{2,1,3,0:T(8,128)} %get-tuple-element.17, f32[8,3,128]{2,1,0:T(4,128)S(1)} %get-tuple-element.13, f32[128,8,3]{0,2,1:T(4,128)S(1)} %get-tuple-element.6, f32[128,8,3]{0,2,1:T(4,128)S(1)} %get-tuple-element.11), kind=kOutput, calls=%fused_computation.34 | convolution fusion | flops 824573952 | bytes 28086272 | tf_op jit(solution)/shard_map/grtn,ngd->grtd/dot_general | solution.py:53
  136.6 0.4 fusion.33
  137.0 354.9 %all-gather.13.cloned.1.call-done = bf16[256,6,1536]{2,1,0:T(8,128)(2,1)} async-done(((bf16[1,6,1536]{2,1,0:T(8,128)(2,1)}), bf16[256,6,1536]{2,1,0:T(8,128)(2,1)}) %all-gather.13.cloned.1.call-update) | async-done | bytes 4718608 | tf_op jit(solution)/shard_map/all_gather | solution.py:80
  491.9 8.4 reshape.176
  500.4 3.2 multiply_reduce_fusion
  503.6 3.6 convolution_convert_fusion.1
  507.2 9.9 %all-to-all-start = ((bf16[32,48,1536]{2,1,0:T(8,128)(2,1)}), bf16[32,48,1536]{2,1,0:T(8,128)(2,1)}, u32[]{:S(2)}, u32[]{:S(2)}) async-start(bf16[32,48,1536]{2,1,0:T(8,128)(2,1)} %bitcast.135), calls=%async_computation | async-start | bytes 9437184 | tf_op jit(solution)/shard_map/all_to_all | solution.py:102
  517.2 0.5 all-gather.7.cloned.1.call-update
  517.7 0.5 all-gather.9.cloned.1.call-update
  518.3 160.1 %all-gather.7.cloned.1.call-done = bf16[1,1536,1024]{2,1,0:T(8,128)(2,1)} async-done(((bf16[1,192,1024]{2,1,0:T(8,128)(2,1)}), bf16[1,1536,1024]{2,1,0:T(8,128)(2,1)}) %all-gather.7.cloned.1.call-update) | async-done | bytes 3145744 | tf_op jit(solution)/shard_map/all_gather | solution.py:107
  678.4 9.8 %convolution_bitcast_fusion = f32[1,1536,1024]{2,1,0:T(8,128)} fusion(bf16[1536,1536]{1,0:T(8,128)(2,1)} %bitcast.29, bf16[1,1536,1024]{2,1,0:T(8,128)(2,1)} %all-gather.7.cloned.1.call-done), kind=kOutput, calls=%fused_computation.16 | convolution fusion | flops 4831838208 | bytes 14155776 | tf_op jit(solution)/shard_map/erd,edf->erf/dot_general | solution.py:104
  688.2 35.5 %all-gather.9.cloned.1.call-done = bf16[1,512,1536]{2,1,0:T(8,128)(2,1)} async-done(((bf16[1,64,1536]{2,1,0:T(8,128)(2,1)}), bf16[1,512,1536]{2,1,0:T(8,128)(2,1)}) %all-gather.9.cloned.1.call-update) | async-done | bytes 1572880 | tf_op jit(solution)/shard_map/all_gather | solution.py:115
  723.7 6.0 fusion.5
  729.7 52.2 %copy.124 = bf16[1,1536,1536]{2,0,1:T(2,128)(2,1)} copy(bf16[1,1536,1536]{2,1,0:T(8,128)(2,1)S(1)} %fusion.5) | data formatting | bytes 9437184 | tf_op jit(solution)/shard_map/convert_element_type | solution.py:117
  781.8 0.5 broadcast.126
  782.4 32.0 %reduce = bf16[1536,1536]{1,0:T(8,128)(2,1)} reduce(bf16[1536,1,1536]{2,1,0:T(2,128)(2,1)} %bitcast.136, bf16[]{:T(256)} %broadcast.126), dimensions={1}, to_apply=%bitcast.134.reduce_sub_computation | reduce | bytes 9437186
  814.3 8.2 reshape.181
  822.5 11.0 %all-to-all-start.1 = ((bf16[32,2,36864]{2,1,0:T(2,128)(2,1)}), bf16[32,2,36864]{2,1,0:T(2,128)(2,1)}, u32[]{:S(2)}, u32[]{:S(2)}) async-start(bf16[32,2,36864]{2,1,0:T(2,128)(2,1)} %reshape.181), calls=%async_computation.1 | async-start | bytes 9437184 | tf_op jit(solution)/shard_map/all_to_all | solution.py:118
  833.5 0.1 copy.103
  833.6 0.3 fusion.51
  834.0 0.1 copy.104
  834.1 2.1 select_reduce_fusion
  836.2 104.9 %all-to-all-done.1 = bf16[32,2,36864]{2,1,0:T(2,128)(2,1)} async-done(((bf16[32,2,36864]{2,1,0:T(2,128)(2,1)}), bf16[32,2,36864]{2,1,0:T(2,128)(2,1)}, u32[]{:S(2)}, u32[]{:S(2)}) %all-to-all-start.1) | async-done | bytes 4718624 | tf_op jit(solution)/shard_map/all_to_all | solution.py:118
  941.0 20.2 %reshape.182 = bf16[1536,1,1536]{2,1,0:T(2,128)(2,1)} reshape(bf16[32,2,36864]{2,1,0:T(2,128)(2,1)} %all-to-all-done.1) | data formatting | bytes 9437184
  961.2 5.2 fusion.14
  (33 shorter events, 0.7 us)
Async XLA Ops:
  7.4 826.2 %copy-start = (bf16[1536,32]{0,1:T(8,128)(2,1)S(1)}, bf16[1536,32]{0,1:T(8,128)(2,1)}, u32[]{:S(2)}) copy-start(bf16[1536,32]{0,1:T(8,128)(2,1)} %param.18) | copy-start | bytes 294916
  7.4 24.0 %copy-start.6 = (s32[1,128]{1,0:T(1,128)S(1)}, s32[1,128]{1,0:T(1,128)}, u32[]{:S(2)}) copy-start(s32[1,128]{1,0:T(1,128)} %param.15) | copy-start | bytes 1540
  7.4 68.1 %all-gather.11.cloned.1.call-start = ((), (), s32[]{:S(2)}) async-start(), calls=%async_computation.4 | async-start | bytes 4325376 | tf_op jit(solution)/shard_map/all_gather | solution.py:66
  8.1 483.8 %all-gather.13.cloned.1.call-start = ((), (), s32[]{:S(2)}) async-start(), calls=%async_computation.5 | async-start | bytes 6316032 | tf_op jit(solution)/shard_map/all_gather | solution.py:80
  105.0 10.2 %copy-start.2 = (f32[8,3,128,128]{2,3,1,0:T(8,128)S(1)}, f32[8,3,128,128]{2,3,1,0:T(8,128)}, u32[]{:S(2)}) copy-start(f32[8,3,128,128]{2,3,1,0:T(8,128)} %get-tuple-element.15) | copy-start | bytes 4718596
  115.4 10.7 %copy-start.1 = (bf16[2048,1,512]{0,2,1:T(8,128)(2,1)S(1)}, bf16[2048,1,512]{0,2,1:T(8,128)(2,1)}, u32[]{:S(2)}) copy-start(bf16[2048,1,512]{0,2,1:T(8,128)(2,1)} %copy.93) | copy-start | bytes 6291460
  137.0 363.3 %copy-start.3 = (bf16[128,1536]{1,0:T(8,128)(2,1)S(1)}, bf16[128,1536]{1,0:T(8,128)(2,1)}, u32[]{:S(2)}) copy-start(bf16[128,1536]{1,0:T(8,128)(2,1)} %param.11) | copy-start | bytes 1179652
  500.3 3.3 copy-start.5
  507.2 171.2 %all-to-all-start = ((bf16[32,48,1536]{2,1,0:T(8,128)(2,1)}), bf16[32,48,1536]{2,1,0:T(8,128)(2,1)}, u32[]{:S(2)}, u32[]{:S(2)}) async-start(bf16[32,48,1536]{2,1,0:T(8,128)(2,1)} %bitcast.135), calls=%async_computation | async-start | bytes 9437184 | tf_op jit(solution)/shard_map/all_to_all | solution.py:102
  517.1 161.3 %all-gather.7.cloned.1.call-start = ((), (), s32[]{:S(2)}) async-start(), calls=%async_computation.2 | async-start | bytes 3538944 | tf_op jit(solution)/shard_map/all_gather | solution.py:107
  517.7 206.0 %all-gather.9.cloned.1.call-start = ((), (), s32[]{:S(2)}) async-start(), calls=%async_computation.3 | async-start | bytes 1769472 | tf_op jit(solution)/shard_map/all_gather | solution.py:115
  822.5 11.4 %copy-start.4 = (s32[128,8]{0,1:T(8,128)S(1)}, s32[128,8]{0,1:T(8,128)}, u32[]{:S(2)}) copy-start(s32[128,8]{0,1:T(8,128)} %param.19) | copy-start | bytes 12292
  822.5 118.6 %all-to-all-start.1 = ((bf16[32,2,36864]{2,1,0:T(2,128)(2,1)}), bf16[32,2,36864]{2,1,0:T(2,128)(2,1)}, u32[]{:S(2)}, u32[]{:S(2)}) async-start(bf16[32,2,36864]{2,1,0:T(2,128)(2,1)} %reshape.181), calls=%async_computation.1 | async-start | bytes 9437184 | tf_op jit(solution)/shard_map/all_to_all | solution.py:118
Sparse Core Ops, SparseCore 0:
  10.7 64.6 all-gather.10
  77.4 414.5 all-gather.12
Sparse Core Ops, SparseCore 1:
  519.4 159.0 all-gather.6
  680.1 43.6 all-gather.8
where the time goes:
time: 976 us; the launch traced here: 974 us
  waiting for transfers between devices  700 us (72%)
  local copies, waits for them, and re-layouts  124 us (13%)
  other arithmetic  63.1 us (6%)
  matrix products  50.7 us (5%)
  starting transfers between devices  21 us (2%)
  between operations  15.1 us (2%)
    all_gather x1, waiting for transfers between devices, per_device(): lax.all_gather(o_weight, ('grp', 'dev'), axis=0, tiled=True)  355 us
    all_gather x1, waiting for transfers between devices, per_device(): lax.all_gather(w_gate_up, 'grp', axis=1, tiled=True)  160 us
    all_to_all x1, waiting for transfers between devices, per_device(): lax.all_to_all(expert_out, 'dev', split_axis=1, concat_axis=0, tiled=True)  105 us
    convert_element_type x1, local copies, waits for them, and re-layouts, per_device(): expert_out = jnp.einsum('erf,efd->erd', sliced, lax.all_gather(w_down, 'g...  52.2 us
    all_gather x1, waiting for transfers between devices, per_device(): piece = lax.all_gather(prefix_kv[0], 'dev', axis=0, tiled=True)  42.5 us
    unnamed x20, local copies, waits for them, and re-layouts  39.3 us
    all_gather x1, waiting for transfers between devices, per_device(): lax.all_gather(w_down, 'grp', axis=1, tiled=True)  35.5 us
    unnamed x1, other arithmetic  32 us
  transfers between devices with their start and end apart: 6, of which 5 were waited for; matrix products, arithmetic and copies ran while one was open for 10% of the time, Pallas kernels for 0%

commit v1 on v0

--- a/solution.py
+++ b/solution.py
@@ -104,7 +104,9 @@
     gate_up = jnp.einsum(
         "erd,edf->erf",
         sliced,
-        lax.all_gather(w_gate_up, "grp", axis=1, tiled=True),
+        jnp.concatenate(
+            lax.all_to_all(jnp.stack([w_gate_up] * lax.axis_size("grp")), "grp", 0, 0), axis=1
+        ),
         preferred_element_type=jnp.float32,
     )
     act = (jax.nn.silu(gate_up[..., :FFE]) * gate_up[..., FFE:]).astype(jnp.bfloat16)

time: 976 us -> 917 us (0.940)
  waiting for transfers between devices: 700 us -> 642 us
    all_gather x1 -> x0, waiting for transfers between devices: 160 us -> none  [per_device(): lax.all_gather(w_gate_up, 'grp', axis=1, tiled=True)]
    all_to_all x1, waiting for transfers between devices: 0.01 us -> 137 us  [per_device(): lax.all_to_all(dispatch, 'dev', split_axis=0, concat_axis=1, tiled=True)]
    all_gather x1, waiting for transfers between devices: 35.5 us -> 0.01 us  [per_device(): lax.all_gather(w_down, 'grp', axis=1, tiled=True)]
    unnamed x20 -> x24, local copies, waits for them, and re-layouts: 39.3 us -> 37.6 us
  transfers between devices with their start and end apart: 6 -> 6, of which waited for: 5 -> 4; matrix products, arithmetic and copies ran while one was open for 10% -> 12% of each run, Pallas kernels for 0% -> 0%
where the time goes in v1:
time: 917 us; the launch traced here: 916 us
  waiting for transfers between devices  642 us (70%)
  local copies, waits for them, and re-layouts  124 us (14%)
  other arithmetic  62.4 us (7%)
  matrix products  50.7 us (6%)
  starting transfers between devices  21.1 us (2%)
  between operations  15.1 us (2%)
    all_gather x1, waiting for transfers between devices, per_device(): lax.all_gather(o_weight, ('grp', 'dev'), axis=0, tiled=True)  354 us
    all_to_all x1, waiting for transfers between devices, per_device(): lax.all_to_all(dispatch, 'dev', split_axis=0, concat_axis=1, tiled=True)  137 us
    all_to_all x1, waiting for transfers between devices, per_device(): lax.all_to_all(expert_out, 'dev', split_axis=1, concat_axis=0, tiled=True)  105 us
    convert_element_type x1, local copies, waits for them, and re-layouts, per_device(): expert_out = jnp.einsum('erf,efd->erd', sliced, lax.all_gather(w_down, 'g...  52.2 us
    all_gather x1, waiting for transfers between devices, per_device(): piece = lax.all_gather(prefix_kv[0], 'dev', axis=0, tiled=True)  44.2 us
    unnamed x24, local copies, waits for them, and re-layouts  37.6 us
    unnamed x1, other arithmetic  32 us
    slice x3, local copies, waits for them, and re-layouts, per_device(): carry = update(initial, piece[:, 0], piece[:, 1], None)  29.5 us
  transfers between devices with their start and end apart: 6, of which 4 were waited for; matrix products, arithmetic and copies ran while one was open for 12% of the time, Pallas kernels for 0%

profile of v1, /device:TPU:1, one launch (start us, length us, event | category | flops | bytes accessed | tf_op | source)
XLA Modules:
  0.0 915.7 jit_solution(992239322473368788)
XLA Ops:
  7.4 0.7 all-gather.8.cloned.1.call-update
  8.1 0.7 all-gather.10.cloned.1.call-update
  8.9 3.2 stack.2
  12.1 6.5 all-to-all-start.1
  18.6 0.1 copy.98
  18.7 0.1 eq.85
  18.8 0.1 eq.81
  18.9 0.2 copy.92
  19.1 0.4 fusion.53
  19.5 0.2 copy.95
  19.7 0.2 copy.96
  19.9 9.0 reduce-window.6
  28.9 0.1 slice.34
  29.0 0.1 copy.100
  29.2 0.1 broadcast_add_fusion
  29.5 8.1 convert_reduce_fusion
  37.6 0.1 fusion.41
  37.7 1.6 fusion.54
  39.3 44.2 %all-gather.8.cloned.1.call-done = bf16[1,2048,2,512]{3,2,0,1:T(2,128)(2,1)} async-done(((bf16[1,64,2,512]{3,2,0,1:T(2,128)(2,1)}), bf16[1,2048,2,512]{3,2,0,1:T(2,128)(2,1)}) %all-gather.8.cloned.1.call-update) | async-done | bytes 4194320 | tf_op jit(solution)/shard_map/all_gather | solution.py:66
  83.5 9.9 %fusion.52 = (bf16[2048,1,512]{2,1,0:T(2,128)(2,1)}, bf16[2048,1,512]{2,1,0:T(2,128)(2,1)}) fusion(bf16[2048,2,512]{2,1,0:T(2,128)(2,1)} %bitcast.137), kind=kLoop, calls=%fused_computation.71 | loop fusion | bytes 8388608 | tf_op jit(solution)/shard_map/slice | solution.py:67
  93.4 10.6 %copy.93 = bf16[2048,1,512]{0,2,1:T(8,128)(2,1)} copy(bf16[2048,1,512]{2,1,0:T(2,128)(2,1)} %get-tuple-element.8) | data formatting | bytes 4194304 | tf_op jit(solution)/shard_map/slice | solution.py:67
  104.0 9.0 copy.91
  113.0 10.1 %bitcast_reduce_fusion = (f32[8,3,128]{2,1,0:T(4,128)S(1)}, f32[8,2048,128,3]{2,1,3,0:T(8,128)}) fusion(bf16[2048,8,64,1]{0,2,3,1:T(8,128)(2,1)S(1)} %bitcast.138, bf16[128,8,3,64]{0,3,2,1:T(8,128)(2,1)S(1)} %bitcast.142), kind=kOutput, calls=%fused_computation.1 | convolution fusion | flops 817886208 | bytes 27668480 | tf_op jit(solution)/shard_map/tgrd,ngd->grtn/dot_general | solution.py:39
  123.2 0.3 fusion.19
  123.5 10.6 %fusion.1 = f32[8,3,128]{2,1,0:T(4,128)S(1)} fusion(f32[8,2048,128,3]{2,1,3,0:T(8,128)} %get-tuple-element.17, f32[8,3,128]{2,1,0:T(4,128)S(1)} %get-tuple-element.13), kind=kLoop, calls=%fused_computation.3 | loop fusion | flops 18871296 | bytes 25190400 | tf_op jit(solution)/shard_map/reduce_sum | solution.py:52
  134.1 10.5 %fusion.29 = f32[128,8,3,64]{0,3,2,1:T(8,128)S(1)} fusion(bf16[2048,8,64,1]{0,2,3,1:T(8,128)(2,1)S(1)} %bitcast.140, f32[8,2048,128,3]{2,1,3,0:T(8,128)} %get-tuple-element.17, f32[8,3,128]{2,1,0:T(4,128)S(1)} %get-tuple-element.13, f32[128,8,3]{0,2,1:T(4,128)S(1)} %get-tuple-element.6, f32[128,8,3]{0,2,1:T(4,128)S(1)} %get-tuple-element.11), kind=kOutput, calls=%fused_computation.33 | convolution fusion | flops 824573952 | bytes 28086272 | tf_op jit(solution)/shard_map/grtn,ngd->grtd/dot_general | solution.py:53
  144.6 0.4 fusion.32
  145.0 354.5 %all-gather.10.cloned.1.call-done = bf16[256,6,1536]{2,1,0:T(8,128)(2,1)} async-done(((bf16[1,6,1536]{2,1,0:T(8,128)(2,1)}), bf16[256,6,1536]{2,1,0:T(8,128)(2,1)}) %all-gather.10.cloned.1.call-update) | async-done | bytes 4718608 | tf_op jit(solution)/shard_map/all_gather | solution.py:80
  499.5 8.4 reshape.181
  507.9 3.2 multiply_reduce_fusion
  511.2 3.6 convolution_convert_fusion.1
  514.8 9.8 %all-to-all-start = ((bf16[32,48,1536]{2,1,0:T(8,128)(2,1)}), bf16[32,48,1536]{2,1,0:T(8,128)(2,1)}, u32[]{:S(2)}, u32[]{:S(2)}) async-start(bf16[32,48,1536]{2,1,0:T(8,128)(2,1)} %bitcast.135), calls=%async_computation | async-start | bytes 9437184 | tf_op jit(solution)/shard_map/all_to_all | solution.py:102
  524.7 0.5 all-gather.6.cloned.1.call-update
  525.2 136.8 %all-to-all-done = bf16[32,48,1536]{2,1,0:T(8,128)(2,1)} async-done(((bf16[32,48,1536]{2,1,0:T(8,128)(2,1)}), bf16[32,48,1536]{2,1,0:T(8,128)(2,1)}, u32[]{:S(2)}, u32[]{:S(2)}) %all-to-all-start) | async-done | bytes 4718624 | tf_op jit(solution)/shard_map/all_to_all | solution.py:102
  662.0 9.8 %convolution_bitcast_fusion = f32[1,1536,1024]{2,1,0:T(8,128)} fusion(bf16[1536,1536]{1,0:T(8,128)(2,1)} %bitcast.29, bf16[1536,1024]{1,0:T(8,128)(2,1)} %bitcast.31), kind=kOutput, calls=%fused_computation.16 | convolution fusion | flops 4831838208 | bytes 14155776 | tf_op jit(solution)/shard_map/erd,edf->erf/dot_general | solution.py:104
  671.8 6.0 fusion.5
  677.8 52.2 %copy.124 = bf16[1,1536,1536]{2,0,1:T(2,128)(2,1)} copy(bf16[1,1536,1536]{2,1,0:T(8,128)(2,1)S(1)} %fusion.5) | data formatting | bytes 9437184 | tf_op jit(solution)/shard_map/convert_element_type | solution.py:119
  729.9 0.5 broadcast.129
  730.5 32.0 %reduce = bf16[1536,1536]{1,0:T(8,128)(2,1)} reduce(bf16[1536,1,1536]{2,1,0:T(2,128)(2,1)} %bitcast.136, bf16[]{:T(256)} %broadcast.129), dimensions={1}, to_apply=%bitcast.134.reduce_sub_computation | reduce | bytes 9437186
  762.4 8.2 reshape.186
  770.6 4.7 all-to-all-start.2
  775.3 0.1 copy.103
  775.4 0.3 fusion.50
  775.8 0.1 copy.104
  775.9 2.1 select_reduce_fusion
  778.0 104.8 %all-to-all-done.2 = bf16[32,2,36864]{2,1,0:T(2,128)(2,1)} async-done(((bf16[32,2,36864]{2,1,0:T(2,128)(2,1)}), bf16[32,2,36864]{2,1,0:T(2,128)(2,1)}, u32[]{:S(2)}, u32[]{:S(2)}) %all-to-all-start.2) | async-done | bytes 4718624 | tf_op jit(solution)/shard_map/all_to_all | solution.py:120
  882.8 20.2 %reshape.187 = bf16[1536,1,1536]{2,1,0:T(2,128)(2,1)} reshape(bf16[32,2,36864]{2,1,0:T(2,128)(2,1)} %all-to-all-done.2) | data formatting | bytes 9437184
  903.0 5.2 fusion.13
  (37 shorter events, 0.6 us)
Async XLA Ops:
  7.4 768.1 %copy-start = (bf16[1536,32]{0,1:T(8,128)(2,1)S(1)}, bf16[1536,32]{0,1:T(8,128)(2,1)}, u32[]{:S(2)}) copy-start(bf16[1536,32]{0,1:T(8,128)(2,1)} %param.18) | copy-start | bytes 294916
  7.4 76.1 %all-gather.8.cloned.1.call-start = ((), (), s32[]{:S(2)}) async-start(), calls=%async_computation.4 | async-start | bytes 4325376 | tf_op jit(solution)/shard_map/all_gather | solution.py:66
  8.1 491.4 %all-gather.10.cloned.1.call-start = ((), (), s32[]{:S(2)}) async-start(), calls=%async_computation.5 | async-start | bytes 6316032 | tf_op jit(solution)/shard_map/all_gather | solution.py:80
  8.8 9.7 %copy-start.6 = (s32[128,8]{0,1:T(8,128)S(1)}, s32[128,8]{0,1:T(8,128)}, u32[]{:S(2)}) copy-start(s32[128,8]{0,1:T(8,128)} %param.19) | copy-start | bytes 12292
  8.9 10.0 %copy-start.5 = (bf16[128,1536]{1,0:T(8,128)(2,1)S(1)}, bf16[128,1536]{1,0:T(8,128)(2,1)}, u32[]{:S(2)}) copy-start(bf16[128,1536]{1,0:T(8,128)(2,1)} %param.12) | copy-start | bytes 1179652
  8.9 10.2 %copy-start.3 = (bf16[128,2,512]{2,1,0:T(2,128)(2,1)S(1)}, bf16[128,2,512]{2,1,0:T(2,128)(2,1)}, u32[]{:S(2)}) copy-start(bf16[128,2,512]{2,1,0:T(2,128)(2,1)} %param.13) | copy-start | bytes 786436
  12.1 25.5 %copy-start.8 = (s32[1,128]{1,0:T(1,128)S(1)}, s32[1,128]{1,0:T(1,128)}, u32[]{:S(2)}) copy-start(s32[1,128]{1,0:T(1,128)} %param.15) | copy-start | bytes 1540
  12.1 502.7 %all-to-all-start.1 = ((bf16[8,1,192,1024]{3,2,1,0:T(8,128)(2,1)}), bf16[8,1,192,1024]{3,2,1,0:T(8,128)(2,1)}, u32[]{:S(2)}, u32[]{:S(2)}) async-start(bf16[8,1,192,1024]{3,2,1,0:T(8,128)(2,1)} %stack.2), calls=%async_computation.1 | async-start | bytes 6291456 | tf_op jit(solution)/shard_map/all_to_all | solution.py:108
  113.0 10.2 %copy-start.2 = (f32[8,3,128,128]{2,3,1,0:T(8,128)S(1)}, f32[8,3,128,128]{2,3,1,0:T(8,128)}, u32[]{:S(2)}) copy-start(f32[8,3,128,128]{2,3,1,0:T(8,128)} %get-tuple-element.15) | copy-start | bytes 4718596
  123.4 10.7 %copy-start.1 = (bf16[2048,1,512]{0,2,1:T(8,128)(2,1)S(1)}, bf16[2048,1,512]{0,2,1:T(8,128)(2,1)}, u32[]{:S(2)}) copy-start(bf16[2048,1,512]{0,2,1:T(8,128)(2,1)} %copy.93) | copy-start | bytes 6291460
  145.0 362.9 %copy-start.4 = (bf16[128,1536]{1,0:T(8,128)(2,1)S(1)}, bf16[128,1536]{1,0:T(8,128)(2,1)}, u32[]{:S(2)}) copy-start(bf16[128,1536]{1,0:T(8,128)(2,1)} %param.11) | copy-start | bytes 1179652
  507.9 3.3 copy-start.7
  514.8 147.2 %all-to-all-start = ((bf16[32,48,1536]{2,1,0:T(8,128)(2,1)}), bf16[32,48,1536]{2,1,0:T(8,128)(2,1)}, u32[]{:S(2)}, u32[]{:S(2)}) async-start(bf16[32,48,1536]{2,1,0:T(8,128)(2,1)} %bitcast.135), calls=%async_computation | async-start | bytes 9437184 | tf_op jit(solution)/shard_map/all_to_all | solution.py:102
  524.6 147.2 %all-gather.6.cloned.1.call-start = ((), (), s32[]{:S(2)}) async-start(), calls=%async_computation.3 | async-start | bytes 1769472 | tf_op jit(solution)/shard_map/all_gather | solution.py:117
  770.6 112.2 %all-to-all-start.2 = ((bf16[32,2,36864]{2,1,0:T(2,128)(2,1)}), bf16[32,2,36864]{2,1,0:T(2,128)(2,1)}, u32[]{:S(2)}, u32[]{:S(2)}) async-start(bf16[32,2,36864]{2,1,0:T(2,128)(2,1)} %reshape.186), calls=%async_computation.2 | async-start | bytes 9437184 | tf_op jit(solution)/shard_map/all_to_all | solution.py:120
Sparse Core Ops, SparseCore 0:
  10.7 72.6 all-gather.7
  85.4 414.0 all-gather.9
Sparse Core Ops, SparseCore 1:
  526.9 112.2 all-gather.5
